TPU v7x, 32 devices: a whole 2x2x4 slice. The times are simulated.
32 devices in a mesh: section: 4 (over y, x), rep: 8 (over z, core).
Axes of the slice: x: 2, y: 2, z: 4, core: 2. Of those that a mesh axis runs over, the one named last changes fastest.
Arguments:
- x_in: bfloat16 [1024, 4096], P('rep'), may hold values from -6 to 6
- cot: bfloat16 [1024, 4096], P('rep'), may hold values from -6 to 6
- w_q: bfloat16 [4, 4096, 128], P('section', 'rep'), may hold values from -0.09375 to 0.09375
- w_k: bfloat16 [4, 4096, 128], P('section', 'rep'), may hold values from -0.09375 to 0.09375
- w_v: bfloat16 [4, 4096, 128], P('section', 'rep'), may hold values from -0.09375 to 0.09375
- w_out: bfloat16 [4, 4096, 128], P('section', 'rep'), may hold values from -0.5 to 0.5
- gains: float32 [4, 4096], P('section'), may hold values from 0.5 to 1.5
- offsets: int32 [4, 8], replicated, may hold values from 0 to 7
- counts: int32 [4, 8], replicated, may hold values from 1 to 8
Outputs:
- grad_q: float32 [4, 4096, 128], P('section', 'rep')
- grad_k: float32 [4, 4096, 128], P('section', 'rep')
- grad_v: float32 [4, 4096, 128], P('section', 'rep')
- grad_o: float32 [4, 4096, 128], P('section', 'rep')
All inputs are finite; a program needn't handle non-finite values.
Results may differ from a plain program's by a relative error of at most 0.023.
Values may be sent and summed in bfloat16 or wider, within the bound.
A program may use at most 64 MiB of HBM per device.

v0:
```python
import jax
import jax.numpy as jnp
from jax import lax
from jax.sharding import PartitionSpec as P

MB = 8
ROWS = 16
EPSILON = 1e-05


def from_behind(block, axis, distance):
    devices = range(lax.axis_size(axis))
    route = [(i - distance, i) for i in devices if i - distance in devices]
    return lax.ppermute(block, axis, route)


def attend(query, key, scale):
    rows_here = query.shape[0]
    scores = jnp.einsum("id,jd->ij", query, key, preferred_element_type=jnp.float32) * scale
    causal = jnp.arange(rows_here)[:, None] >= jnp.arange(rows_here)[None, :]
    expo = jnp.exp(jnp.where(causal, scores, -1e30))
    return expo / jnp.sum(expo, axis=-1, keepdims=True)


def forward_layer(layer_in, gain, weights, keep):
    weight_q, weight_k, weight_v, weight_o = weights
    scale = weight_q.shape[1] ** (-0.5)
    x_float = layer_in.astype(jnp.float32)
    rinv = lax.rsqrt(jnp.mean(x_float * x_float, axis=-1, keepdims=True) + EPSILON)
    normed = (x_float * rinv * gain).astype(jnp.bfloat16)
    query = jnp.dot(normed, weight_q, preferred_element_type=jnp.float32).astype(jnp.bfloat16)
    key = jnp.dot(normed, weight_k, preferred_element_type=jnp.float32).astype(jnp.bfloat16)
    value = jnp.dot(normed, weight_v, preferred_element_type=jnp.float32).astype(jnp.bfloat16)
    probs_low = attend(query, key, scale).astype(jnp.bfloat16)
    heads = jnp.dot(probs_low, value, preferred_element_type=jnp.float32).astype(jnp.bfloat16)
    output = lax.dot_general(
        heads, weight_o, (((1,), (1,)), ((), ())), preferred_element_type=jnp.float32
    )
    result = (x_float + keep * output).astype(jnp.bfloat16)
    return (result, normed, query, key, value, heads)


def backward_layer(grad_in, layer_in, query, key, value, gain, weights, keep):
    weight_q, weight_k, weight_v, weight_o = weights
    scale = weight_q.shape[1] ** (-0.5)
    grad_float = grad_in.astype(jnp.float32)
    grad_rows = (keep * grad_float).astype(jnp.bfloat16)
    d_heads = jnp.dot(grad_rows, weight_o, preferred_element_type=jnp.float32).astype(jnp.bfloat16)
    probs = attend(query, key, scale)
    probs_low = probs.astype(jnp.bfloat16)
    d_value = jnp.einsum(
        "ij,id->jd", probs_low, d_heads, preferred_element_type=jnp.float32
    ).astype(jnp.bfloat16)
    d_probs = jnp.einsum("id,jd->ij", d_heads, value, preferred_element_type=jnp.float32)
    d_score = (probs * (d_probs - jnp.sum(probs * d_probs, axis=-1, keepdims=True)) * scale).astype(
        jnp.bfloat16
    )
    d_query = jnp.dot(d_score, key, preferred_element_type=jnp.float32).astype(jnp.bfloat16)
    d_key = jnp.einsum("ij,id->jd", d_score, query, preferred_element_type=jnp.float32).astype(
        jnp.bfloat16
    )
    contract = (((1,), (1,)), ((), ()))
    d_normed = lax.dot_general(d_query, weight_q, contract, preferred_element_type=jnp.float32)
    d_normed = d_normed + lax.dot_general(
        d_key, weight_k, contract, preferred_element_type=jnp.float32
    )
    d_normed = d_normed + lax.dot_general(
        d_value, weight_v, contract, preferred_element_type=jnp.float32
    )
    x_float = layer_in.astype(jnp.float32)
    rinv = lax.rsqrt(jnp.mean(x_float * x_float, axis=-1, keepdims=True) + EPSILON)
    scaled = d_normed * gain
    d_input = rinv * (
        scaled - x_float * rinv * rinv * jnp.mean(scaled * x_float, axis=-1, keepdims=True)
    )
    return ((grad_float + d_input).astype(jnp.bfloat16), grad_rows, d_query, d_key, d_value)


def store_slot(store, value, slot_at, is_valid):
    old_value = lax.dynamic_index_in_dim(store, slot_at, 0, keepdims=False)
    fresh = jnp.where(is_valid, value, old_value)
    return lax.dynamic_update_index_in_dim(store, fresh, slot_at, 0)


def zeros_like_all(values):
    return tuple((jnp.zeros(value.shape, value.dtype) for value in values))


def pick_slot(store, slot_at):
    return lax.dynamic_index_in_dim(store, slot_at, 0, keepdims=False)


def local_grad(left, right):
    width_left = left.shape[-1]
    width_right = right.shape[-1]
    return jnp.einsum(
        "td,th->dh",
        left.reshape(-1, width_left),
        right.reshape(-1, width_right),
        preferred_element_type=jnp.float32,
    )


def on_device(x_in, cot, w_q, w_k, w_v, w_out, gains, offsets, counts):
    section_count = lax.axis_size("section")
    rep_count = lax.axis_size("rep")
    section_pos = lax.axis_index("section")
    rep_pos = lax.axis_index("rep")
    weights = (
        lax.all_gather(w_q[0], "rep", axis=0, tiled=True),
        lax.all_gather(w_k[0], "rep", axis=0, tiled=True),
        lax.all_gather(w_v[0], "rep", axis=0, tiled=True),
        lax.all_gather(w_out[0], "rep", axis=0, tiled=True),
    )
    width = weights[0].shape[0]
    head_size = weights[0].shape[1]
    gain = gains[0]
    landing_sum = jnp.cumsum(offsets, axis=0) % rep_count
    my_offsets = lax.dynamic_index_in_dim(landing_sum, section_pos, 0, keepdims=False)
    landing = (rep_pos + my_offsets) % rep_count
    count_row = lax.dynamic_index_in_dim(counts, section_pos, 0, keepdims=False)
    match_rep = landing[:, None] == jnp.arange(rep_count, dtype=jnp.int32)[None, :]
    allowed = jnp.sum(jnp.where(match_rep, count_row[None, :], 0), axis=1)
    keeps = (jnp.arange(MB, dtype=jnp.int32) < allowed).astype(jnp.float32)
    inputs = x_in.reshape(MB, ROWS, width)
    top_grads = cot.reshape(MB, ROWS, width)
    tick_count = section_count + MB - 1
    row_block = jnp.zeros((ROWS, width), jnp.bfloat16)
    head_block = jnp.zeros((ROWS, head_size), jnp.bfloat16)

    def forward_tick(tick_no, carry):
        inbox, saved_in, saved_normed, saved_q, saved_k, saved_v, saved_heads = carry
        batch_pos = tick_no - section_pos
        is_valid = (batch_pos >= 0) & (batch_pos < MB)
        batch_at = jnp.clip(batch_pos, 0, MB - 1)
        own_rows = pick_slot(inputs, batch_at)
        layer_in = jnp.where(section_pos == 0, own_rows, inbox)
        keep = pick_slot(keeps, batch_at)
        blank = (row_block, row_block, head_block, head_block, head_block, head_block)
        made = lax.cond(
            is_valid,
            lambda rows_in: forward_layer(rows_in, gain, weights, keep),
            lambda rows_in: zeros_like_all(blank),
            layer_in,
        )
        result, normed, query, key, value, heads = made
        saved_in = store_slot(saved_in, layer_in, batch_at, is_valid)
        saved_normed = store_slot(saved_normed, normed, batch_at, is_valid)
        saved_q = store_slot(saved_q, query, batch_at, is_valid)
        saved_k = store_slot(saved_k, key, batch_at, is_valid)
        saved_v = store_slot(saved_v, value, batch_at, is_valid)
        saved_heads = store_slot(saved_heads, heads, batch_at, is_valid)
        inbox = from_behind(result, "section", 1)
        return (inbox, saved_in, saved_normed, saved_q, saved_k, saved_v, saved_heads)

    wide_store = jnp.zeros((MB, ROWS, width), jnp.bfloat16)
    head_store = jnp.zeros((MB, ROWS, head_size), jnp.bfloat16)
    start_fwd = (row_block, wide_store, wide_store, head_store, head_store, head_store, head_store)
    _, saved_in, saved_normed, saved_q, saved_k, saved_v, saved_heads = lax.fori_loop(
        0, tick_count, forward_tick, start_fwd
    )

    def backward_tick(tick_no, carry):
        inbox, saved_rows, saved_dq, saved_dk, saved_dv = carry
        batch_pos = tick_no - (section_count - 1 - section_pos)
        is_valid = (batch_pos >= 0) & (batch_pos < MB)
        batch_at = jnp.clip(batch_pos, 0, MB - 1)
        grad_in = jnp.where(section_pos == section_count - 1, pick_slot(top_grads, batch_at), inbox)
        layer_in = pick_slot(saved_in, batch_at)
        query = pick_slot(saved_q, batch_at)
        key = pick_slot(saved_k, batch_at)
        value = pick_slot(saved_v, batch_at)
        keep = pick_slot(keeps, batch_at)
        blank = (row_block, row_block, head_block, head_block, head_block)
        made = lax.cond(
            is_valid,
            lambda rows_in: backward_layer(
                rows_in, layer_in, query, key, value, gain, weights, keep
            ),
            lambda rows_in: zeros_like_all(blank),
            grad_in,
        )
        grad_back, grad_rows, d_query, d_key, d_value = made
        saved_rows = store_slot(saved_rows, grad_rows, batch_at, is_valid)
        saved_dq = store_slot(saved_dq, d_query, batch_at, is_valid)
        saved_dk = store_slot(saved_dk, d_key, batch_at, is_valid)
        saved_dv = store_slot(saved_dv, d_value, batch_at, is_valid)
        inbox = from_behind(grad_back, "section", -1)
        return (inbox, saved_rows, saved_dq, saved_dk, saved_dv)

    start_bwd = (row_block, wide_store, head_store, head_store, head_store)
    _, saved_rows, saved_dq, saved_dk, saved_dv = lax.fori_loop(
        0, tick_count, backward_tick, start_bwd
    )
    full_q = local_grad(saved_normed, saved_dq)
    full_k = local_grad(saved_normed, saved_dk)
    full_v = local_grad(saved_normed, saved_dv)
    full_o = local_grad(saved_rows, saved_heads)
    share_width = width // rep_count
    totals = (
        lax.psum(full_q.astype(jnp.bfloat16), "rep").astype(jnp.float32),
        lax.psum(full_k.astype(jnp.bfloat16), "rep").astype(jnp.float32),
        lax.psum(full_v.astype(jnp.bfloat16), "rep").astype(jnp.float32),
        lax.psum(full_o.astype(jnp.bfloat16), "rep").astype(jnp.float32),
    )
    parts = tuple(
        (lax.dynamic_slice_in_dim(total, rep_pos * share_width, share_width, 0) for total in totals)
    )
    return (parts[0][None], parts[1][None], parts[2][None], parts[3][None])


def solution(mesh):
    in_specs = (
        P("rep", None),
        P("rep", None),
        P("section", "rep", None),
        P("section", "rep", None),
        P("section", "rep", None),
        P("section", "rep", None),
        P("section", None),
        P(),
        P(),
    )
    out_specs = (
        P("section", "rep", None),
        P("section", "rep", None),
        P("section", "rep", None),
        P("section", "rep", None),
    )
    return jax.shard_map(
        on_device, mesh=mesh, in_specs=in_specs, out_specs=out_specs, check_vma=False
    )
```

profile of v0, /device:TPU:0, one launch (start us, length us, event | category | flops | bytes accessed | tf_op | source)
XLA Modules:
  0.0 682.0 jit_solution(16594448629739413946)
XLA Ops:
  11.5 23.1 %all-gather.9.cloned.1.call-done = bf16[1,4096,128]{2,1,0:T(8,128)(2,1)} async-done(((bf16[1,512,128]{2,1,0:T(8,128)(2,1)}), bf16[1,4096,128]{2,1,0:T(8,128)(2,1)}) %all-gather.9.cloned.1.call-update) | async-done | bytes 1048592 | tf_op jit(solution)/shard_map/all_gather | solution.py:110
  34.6 23.5 %all-gather.11.cloned.1.call-done = bf16[1,4096,128]{2,1,0:T(8,128)(2,1)} async-done(((bf16[1,512,128]{2,1,0:T(8,128)(2,1)}), bf16[1,4096,128]{2,1,0:T(8,128)(2,1)}) %all-gather.11.cloned.1.call-update) | async-done | bytes 1048592 | tf_op jit(solution)/shard_map/all_gather | solution.py:111
  58.1 23.5 %all-gather.13.cloned.1.call-done = bf16[1,4096,128]{2,1,0:T(8,128)(2,1)} async-done(((bf16[1,512,128]{2,1,0:T(8,128)(2,1)}), bf16[1,4096,128]{2,1,0:T(8,128)(2,1)}) %all-gather.13.cloned.1.call-update) | async-done | bytes 1048592 | tf_op jit(solution)/shard_map/all_gather | solution.py:112
  81.6 23.3 %all-gather.15.cloned.1.call-done = bf16[1,4096,128]{2,1,0:T(8,128)(2,1)} async-done(((bf16[1,512,128]{2,1,0:T(8,128)(2,1)}), bf16[1,4096,128]{2,1,0:T(8,128)(2,1)}) %all-gather.15.cloned.1.call-update) | async-done | bytes 1048592 | tf_op jit(solution)/shard_map/all_gather | solution.py:113
  109.6 211.7 %while.49 = (s32[]{:T(128)}, bf16[16,4096]{1,0:T(8,128)(2,1)S(1)}, bf16[8,16,4096]{2,1,0:T(8,128)(2,1)}, bf16[8,16,4096]{2,1,0:T(8,128)(2,1)}, bf16[8,16,128]{2,...) while((s32[]{:T(128)}, bf16[16,4096]{1,0:T(8,128)(2,1)S(1)}, ...), condition=%wide.region_7.8_spmd, body=%wide.region_2.7_spmd.sunk | while | flops 68175368 | bytes 16946660 | solution.py:159
  112.2 8.9 %conditional.4 = (bf16[16,4096]{1,0:T(8,128)(2,1)}, bf16[16,4096]{1,0:T(8,128)(2,1)S(1)}, bf16[16,128]{1,0:T(8,128)(2,1)}, bf16[16,128]{1,0:T(8,128)(2,1)S(1)}, ...) conditional(s32[]{:T(128)} %convert_element_type.174, () %tuple.109, (bf16[16,4096]{1,0:T(8,128)(2,1)S(1)}, ...), branch_computations={%region_3.3_spmd, %region_4.6_spmd} | conditional | flops 67970560 | bytes 14764648 | solution.py:140
  118.7 2.3 fusion.1
  131.8 8.9 %conditional.4 = (bf16[16,4096]{1,0:T(8,128)(2,1)}, bf16[16,4096]{1,0:T(8,128)(2,1)S(1)}, bf16[16,128]{1,0:T(8,128)(2,1)}, bf16[16,128]{1,0:T(8,128)(2,1)S(1)}, ...) conditional(s32[]{:T(128)} %convert_element_type.174, () %tuple.109, (bf16[16,4096]{1,0:T(8,128)(2,1)S(1)}, ...), branch_computations={%region_3.3_spmd, %region_4.6_spmd} | conditional | flops 67970560 | bytes 14764648 | solution.py:140
  138.3 2.3 fusion.1
  151.5 8.9 %conditional.4 = (bf16[16,4096]{1,0:T(8,128)(2,1)}, bf16[16,4096]{1,0:T(8,128)(2,1)S(1)}, bf16[16,128]{1,0:T(8,128)(2,1)}, bf16[16,128]{1,0:T(8,128)(2,1)S(1)}, ...) conditional(s32[]{:T(128)} %convert_element_type.174, () %tuple.109, (bf16[16,4096]{1,0:T(8,128)(2,1)S(1)}, ...), branch_computations={%region_3.3_spmd, %region_4.6_spmd} | conditional | flops 67970560 | bytes 14764648 | solution.py:140
  158.0 2.3 fusion.1
  160.3 1.7 collective-permute-start
  171.5 8.9 %conditional.4 = (bf16[16,4096]{1,0:T(8,128)(2,1)}, bf16[16,4096]{1,0:T(8,128)(2,1)S(1)}, bf16[16,128]{1,0:T(8,128)(2,1)}, bf16[16,128]{1,0:T(8,128)(2,1)S(1)}, ...) conditional(s32[]{:T(128)} %convert_element_type.174, () %tuple.109, (bf16[16,4096]{1,0:T(8,128)(2,1)S(1)}, ...), branch_computations={%region_3.3_spmd, %region_4.6_spmd} | conditional | flops 67970560 | bytes 14764648 | solution.py:140
  178.0 2.3 fusion.1
  180.3 1.9 collective-permute-start
  191.8 8.9 %conditional.4 = (bf16[16,4096]{1,0:T(8,128)(2,1)}, bf16[16,4096]{1,0:T(8,128)(2,1)S(1)}, bf16[16,128]{1,0:T(8,128)(2,1)}, bf16[16,128]{1,0:T(8,128)(2,1)S(1)}, ...) conditional(s32[]{:T(128)} %convert_element_type.174, () %tuple.109, (bf16[16,4096]{1,0:T(8,128)(2,1)S(1)}, ...), branch_computations={%region_3.3_spmd, %region_4.6_spmd} | conditional | flops 67970560 | bytes 14764648 | solution.py:140
  198.3 2.3 fusion.1
  200.6 1.9 collective-permute-start
  212.0 8.9 %conditional.4 = (bf16[16,4096]{1,0:T(8,128)(2,1)}, bf16[16,4096]{1,0:T(8,128)(2,1)S(1)}, bf16[16,128]{1,0:T(8,128)(2,1)}, bf16[16,128]{1,0:T(8,128)(2,1)S(1)}, ...) conditional(s32[]{:T(128)} %convert_element_type.174, () %tuple.109, (bf16[16,4096]{1,0:T(8,128)(2,1)S(1)}, ...), branch_computations={%region_3.3_spmd, %region_4.6_spmd} | conditional | flops 67970560 | bytes 14764648 | solution.py:140
  218.5 2.3 fusion.1
  220.9 1.9 collective-permute-start
  232.2 8.9 %conditional.4 = (bf16[16,4096]{1,0:T(8,128)(2,1)}, bf16[16,4096]{1,0:T(8,128)(2,1)S(1)}, bf16[16,128]{1,0:T(8,128)(2,1)}, bf16[16,128]{1,0:T(8,128)(2,1)S(1)}, ...) conditional(s32[]{:T(128)} %convert_element_type.174, () %tuple.109, (bf16[16,4096]{1,0:T(8,128)(2,1)S(1)}, ...), branch_computations={%region_3.3_spmd, %region_4.6_spmd} | conditional | flops 67970560 | bytes 14764648 | solution.py:140
  238.8 2.3 fusion.1
  241.1 1.9 collective-permute-start
  250.9 1.6 bitcast_dynamic-update-slice_fusion.17
  252.5 8.9 %conditional.4 = (bf16[16,4096]{1,0:T(8,128)(2,1)}, bf16[16,4096]{1,0:T(8,128)(2,1)S(1)}, bf16[16,128]{1,0:T(8,128)(2,1)}, bf16[16,128]{1,0:T(8,128)(2,1)S(1)}, ...) conditional(s32[]{:T(128)} %convert_element_type.174, () %tuple.109, (bf16[16,4096]{1,0:T(8,128)(2,1)S(1)}, ...), branch_computations={%region_3.3_spmd, %region_4.6_spmd} | conditional | flops 67970560 | bytes 14764648 | solution.py:140
  259.1 2.3 fusion.1
  261.4 1.9 collective-permute-start
  271.1 1.6 bitcast_dynamic-update-slice_fusion.17
  272.8 2.4 conditional.4
  275.2 8.3 %collective-permute-start = (bf16[16,4096]{1,0:T(8,128)(2,1)}, bf16[16,4096]{1,0:T(8,128)(2,1)S(1)}, u32[]{:S(2)}, u32[]{:S(2)}) collective-permute-start(bf16[16,4096]{1,0:T(8,128)(2,1)} %get-tuple-element.1244), channel_id=1, source_target_pairs={{0,8},{8,16},{16,24},{1,9},{9,17},{17,25},{2,10},{10,18},{18,26},{... | collective-permute-start | bytes 393224 | tf_op jit(solution)/shard_map/while/body/eval_jaxpr/ppermute | solution.py:14
  290.0 1.6 bitcast_dynamic-update-slice_fusion.17
  291.7 2.4 conditional.4
  294.1 3.3 collective-permute-start
  305.5 2.4 conditional.4
  308.0 7.8 %collective-permute-start = (bf16[16,4096]{1,0:T(8,128)(2,1)}, bf16[16,4096]{1,0:T(8,128)(2,1)S(1)}, u32[]{:S(2)}, u32[]{:S(2)}) collective-permute-start(bf16[16,4096]{1,0:T(8,128)(2,1)} %get-tuple-element.1244), channel_id=1, source_target_pairs={{0,8},{8,16},{16,24},{1,9},{9,17},{17,25},{2,10},{10,18},{18,26},{... | collective-permute-start | bytes 393224 | tf_op jit(solution)/shard_map/while/body/eval_jaxpr/ppermute | solution.py:14
  324.3 241.3 %while.50 = (s32[]{:T(128)}, bf16[16,4096]{1,0:T(8,128)(2,1)S(1)}, bf16[8,16,4096]{2,1,0:T(8,128)(2,1)}, bf16[8,16,128]{2,1,0:T(8,128)(2,1)}, bf16[8,16,128]{2,1...) while((s32[]{:T(128)}, bf16[16,4096]{1,0:T(8,128)(2,1)S(1)}, ...), condition=%wide.region_15.16_spmd, body=%wide.region_8.15_spmd.sunk | while | flops 68961784 | bytes 9356268 | solution.py:192
  324.3 1.9 conditional.5
  333.6 1.9 conditional.5
  344.2 1.9 conditional.5
  353.5 33.2 %collective-permute-done.1 = bf16[16,4096]{1,0:T(8,128)(2,1)S(1)} collective-permute-done((bf16[16,4096]{1,0:T(8,128)(2,1)}, bf16[16,4096]{1,0:T(8,128)(2,1)S(1)}, u32[]{:S(2)}, u32[]{:S(2)}) %collective-permute-start.1) | collective-permute-done | bytes 131104 | tf_op jit(solution)/shard_map/while/body/eval_jaxpr/ppermute | solution.py:14
  386.7 13.7 %conditional.5 = (bf16[16,4096]{1,0:T(8,128)(2,1)}, bf16[16,4096]{1,0:T(8,128)(2,1)S(1)}, bf16[16,128]{1,0:T(8,128)(2,1)S(1)}, bf16[16,128]{1,0:T(8,128)(2,1)}, bf16[16,128]{1,0:T(8,128)(2,1)}) conditional(s32[]{:T(128)} %convert_element_type.175, () %tuple.113, (pred[]{:T(512)}, bf16[8,16,4096]{2,1,0:T(8,128)(2,1)}, s32[]{:T(128)}, ...), branch_computations={%region_9.9_spmd, %region_10.14_spmd} | conditional | flops 68890096 | bytes 8113206 | solution.py:175
  398.6 1.8 fusion.12
  409.1 13.7 %conditional.5 = (bf16[16,4096]{1,0:T(8,128)(2,1)}, bf16[16,4096]{1,0:T(8,128)(2,1)S(1)}, bf16[16,128]{1,0:T(8,128)(2,1)S(1)}, bf16[16,128]{1,0:T(8,128)(2,1)}, bf16[16,128]{1,0:T(8,128)(2,1)}) conditional(s32[]{:T(128)} %convert_element_type.175, () %tuple.113, (pred[]{:T(512)}, bf16[8,16,4096]{2,1,0:T(8,128)(2,1)}, s32[]{:T(128)}, ...), branch_computations={%region_9.9_spmd, %region_10.14_spmd} | conditional | flops 68890096 | bytes 8113206 | solution.py:175
  421.0 1.8 fusion.12
  431.6 13.7 %conditional.5 = (bf16[16,4096]{1,0:T(8,128)(2,1)}, bf16[16,4096]{1,0:T(8,128)(2,1)S(1)}, bf16[16,128]{1,0:T(8,128)(2,1)S(1)}, bf16[16,128]{1,0:T(8,128)(2,1)}, bf16[16,128]{1,0:T(8,128)(2,1)}) conditional(s32[]{:T(128)} %convert_element_type.175, () %tuple.113, (pred[]{:T(512)}, bf16[8,16,4096]{2,1,0:T(8,128)(2,1)}, s32[]{:T(128)}, ...), branch_computations={%region_9.9_spmd, %region_10.14_spmd} | conditional | flops 68890096 | bytes 8113206 | solution.py:175
  443.5 1.8 fusion.12
  454.0 13.7 %conditional.5 = (bf16[16,4096]{1,0:T(8,128)(2,1)}, bf16[16,4096]{1,0:T(8,128)(2,1)S(1)}, bf16[16,128]{1,0:T(8,128)(2,1)S(1)}, bf16[16,128]{1,0:T(8,128)(2,1)}, bf16[16,128]{1,0:T(8,128)(2,1)}) conditional(s32[]{:T(128)} %convert_element_type.175, () %tuple.113, (pred[]{:T(512)}, bf16[8,16,4096]{2,1,0:T(8,128)(2,1)}, s32[]{:T(128)}, ...), branch_computations={%region_9.9_spmd, %region_10.14_spmd} | conditional | flops 68890096 | bytes 8113206 | solution.py:175
  465.9 1.8 fusion.12
  476.4 13.7 %conditional.5 = (bf16[16,4096]{1,0:T(8,128)(2,1)}, bf16[16,4096]{1,0:T(8,128)(2,1)S(1)}, bf16[16,128]{1,0:T(8,128)(2,1)S(1)}, bf16[16,128]{1,0:T(8,128)(2,1)}, bf16[16,128]{1,0:T(8,128)(2,1)}) conditional(s32[]{:T(128)} %convert_element_type.175, () %tuple.113, (pred[]{:T(512)}, bf16[8,16,4096]{2,1,0:T(8,128)(2,1)}, s32[]{:T(128)}, ...), branch_computations={%region_9.9_spmd, %region_10.14_spmd} | conditional | flops 68890096 | bytes 8113206 | solution.py:175
  488.4 1.8 fusion.12
  498.9 13.7 %conditional.5 = (bf16[16,4096]{1,0:T(8,128)(2,1)}, bf16[16,4096]{1,0:T(8,128)(2,1)S(1)}, bf16[16,128]{1,0:T(8,128)(2,1)S(1)}, bf16[16,128]{1,0:T(8,128)(2,1)}, bf16[16,128]{1,0:T(8,128)(2,1)}) conditional(s32[]{:T(128)} %convert_element_type.175, () %tuple.113, (pred[]{:T(512)}, bf16[8,16,4096]{2,1,0:T(8,128)(2,1)}, s32[]{:T(128)}, ...), branch_computations={%region_9.9_spmd, %region_10.14_spmd} | conditional | flops 68890096 | bytes 8113206 | solution.py:175
  510.8 1.8 fusion.12
  521.3 13.7 %conditional.5 = (bf16[16,4096]{1,0:T(8,128)(2,1)}, bf16[16,4096]{1,0:T(8,128)(2,1)S(1)}, bf16[16,128]{1,0:T(8,128)(2,1)S(1)}, bf16[16,128]{1,0:T(8,128)(2,1)}, bf16[16,128]{1,0:T(8,128)(2,1)}) conditional(s32[]{:T(128)} %convert_element_type.175, () %tuple.113, (pred[]{:T(512)}, bf16[8,16,4096]{2,1,0:T(8,128)(2,1)}, s32[]{:T(128)}, ...), branch_computations={%region_9.9_spmd, %region_10.14_spmd} | conditional | flops 68890096 | bytes 8113206 | solution.py:175
  533.2 1.8 fusion.12
  543.7 13.7 %conditional.5 = (bf16[16,4096]{1,0:T(8,128)(2,1)}, bf16[16,4096]{1,0:T(8,128)(2,1)S(1)}, bf16[16,128]{1,0:T(8,128)(2,1)S(1)}, bf16[16,128]{1,0:T(8,128)(2,1)}, bf16[16,128]{1,0:T(8,128)(2,1)}) conditional(s32[]{:T(128)} %convert_element_type.175, () %tuple.113, (pred[]{:T(512)}, bf16[8,16,4096]{2,1,0:T(8,128)(2,1)}, s32[]{:T(128)}, ...), branch_computations={%region_9.9_spmd, %region_10.14_spmd} | conditional | flops 68890096 | bytes 8113206 | solution.py:175
  555.7 1.8 fusion.12
  565.6 2.7 fusion.37
  568.3 2.7 fusion.36
  571.0 2.7 fusion.35
  573.7 2.2 fusion.38
  576.0 96.0 %all-reduce.3.cloned.1.call-done = (bf16[4096,128]{1,0:T(8,128)(2,1)}, bf16[4096,128]{1,0:T(8,128)(2,1)}, bf16[4096,128]{1,0:T(8,128)(2,1)}, bf16[4096,128]{1,0:T(8,128)(2,1)}) async-done(((bf16[4096,128]{1,0:T(8,128)(2,1)}, bf16[4096,128]{1,0:T(8,128)(2,1)}, bf16[4096,128]{1,0:T(8,128)(2,1)}, bf16[4096,128]{1,0:T(8,128)(2,1)}), (bf16[4096,128]{1,0:T(8,128)(2,1)}, bf16[4096,128]{1,0:T(8,128)(2,1)}, ...) | async-done | bytes 4194320 | tf_op jit(solution)/shard_map/psum | solution.py:201
  671.9 1.8 convert_bitcast_fusion
  673.7 1.8 convert_bitcast_fusion.2
  (629 shorter events, 362.1 us)
Async XLA Ops:
  7.2 3.6 copy-start
  7.2 27.5 %all-gather.9.cloned.1.call-start = ((), (), s32[]{:S(2)}) async-start(), calls=%async_computation | async-start | bytes 1179648 | tf_op jit(solution)/shard_map/all_gather | solution.py:110
  7.9 50.2 %all-gather.11.cloned.1.call-start = ((), (), s32[]{:S(2)}) async-start(), calls=%async_computation.1 | async-start | bytes 1179648 | tf_op jit(solution)/shard_map/all_gather | solution.py:111
  8.7 72.9 %all-gather.13.cloned.1.call-start = ((), (), s32[]{:S(2)}) async-start(), calls=%async_computation.2 | async-start | bytes 1179648 | tf_op jit(solution)/shard_map/all_gather | solution.py:112
  9.4 95.5 %all-gather.15.cloned.1.call-start = ((), (), s32[]{:S(2)}) async-start(), calls=%async_computation.3 | async-start | bytes 1179648 | tf_op jit(solution)/shard_map/all_gather | solution.py:113
  10.0 661.9 %all-reduce.3.cloned.1.call-start = ((), (), s32[]{:S(2)}) async-start(), calls=%async_computation.4 | async-start | bytes 8388608 | tf_op jit(solution)/shard_map/psum | solution.py:201
  104.9 4.7 copy-start.1
  104.9 4.7 copy-start.2
  113.4 5.3 copy-start.5
  116.0 5.1 copy-start.7
  117.4 3.6 copy-start.14
  121.0 8.2 %collective-permute-start = (bf16[16,4096]{1,0:T(8,128)(2,1)}, bf16[16,4096]{1,0:T(8,128)(2,1)S(1)}, u32[]{:S(2)}, u32[]{:S(2)}) collective-permute-start(bf16[16,4096]{1,0:T(8,128)(2,1)} %get-tuple-element.1244), channel_id=1, source_target_pairs={{0,8},{8,16},{16,24},{1,9},{9,17},{17,25},{2,10},{10,18},{18,26},{... | collective-permute-start | bytes 393224 | tf_op jit(solution)/shard_map/while/body/eval_jaxpr/ppermute | solution.py:14
  133.1 5.3 copy-start.5
  135.6 5.1 copy-start.7
  137.1 3.6 copy-start.14
  140.7 8.2 %collective-permute-start = (bf16[16,4096]{1,0:T(8,128)(2,1)}, bf16[16,4096]{1,0:T(8,128)(2,1)S(1)}, u32[]{:S(2)}, u32[]{:S(2)}) collective-permute-start(bf16[16,4096]{1,0:T(8,128)(2,1)} %get-tuple-element.1244), channel_id=1, source_target_pairs={{0,8},{8,16},{16,24},{1,9},{9,17},{17,25},{2,10},{10,18},{18,26},{... | collective-permute-start | bytes 393224 | tf_op jit(solution)/shard_map/while/body/eval_jaxpr/ppermute | solution.py:14
  152.7 5.3 copy-start.5
  155.2 5.1 copy-start.7
  156.7 3.6 copy-start.14
  160.3 8.6 %collective-permute-start = (bf16[16,4096]{1,0:T(8,128)(2,1)}, bf16[16,4096]{1,0:T(8,128)(2,1)S(1)}, u32[]{:S(2)}, u32[]{:S(2)}) collective-permute-start(bf16[16,4096]{1,0:T(8,128)(2,1)} %get-tuple-element.1244), channel_id=1, source_target_pairs={{0,8},{8,16},{16,24},{1,9},{9,17},{17,25},{2,10},{10,18},{18,26},{... | collective-permute-start | bytes 393224 | tf_op jit(solution)/shard_map/while/body/eval_jaxpr/ppermute | solution.py:14
  172.7 5.3 copy-start.5
  175.3 5.1 copy-start.7
  176.7 3.6 copy-start.14
  180.3 8.9 %collective-permute-start = (bf16[16,4096]{1,0:T(8,128)(2,1)}, bf16[16,4096]{1,0:T(8,128)(2,1)S(1)}, u32[]{:S(2)}, u32[]{:S(2)}) collective-permute-start(bf16[16,4096]{1,0:T(8,128)(2,1)} %get-tuple-element.1244), channel_id=1, source_target_pairs={{0,8},{8,16},{16,24},{1,9},{9,17},{17,25},{2,10},{10,18},{18,26},{... | collective-permute-start | bytes 393224 | tf_op jit(solution)/shard_map/while/body/eval_jaxpr/ppermute | solution.py:14
  193.0 5.3 copy-start.5
  195.6 5.1 copy-start.7
  197.0 3.6 copy-start.14
  200.6 8.8 %collective-permute-start = (bf16[16,4096]{1,0:T(8,128)(2,1)}, bf16[16,4096]{1,0:T(8,128)(2,1)S(1)}, u32[]{:S(2)}, u32[]{:S(2)}) collective-permute-start(bf16[16,4096]{1,0:T(8,128)(2,1)} %get-tuple-element.1244), channel_id=1, source_target_pairs={{0,8},{8,16},{16,24},{1,9},{9,17},{17,25},{2,10},{10,18},{18,26},{... | collective-permute-start | bytes 393224 | tf_op jit(solution)/shard_map/while/body/eval_jaxpr/ppermute | solution.py:14
  213.2 5.3 copy-start.5
  215.8 5.1 copy-start.7
  217.3 3.6 copy-start.14
  220.9 8.8 %collective-permute-start = (bf16[16,4096]{1,0:T(8,128)(2,1)}, bf16[16,4096]{1,0:T(8,128)(2,1)S(1)}, u32[]{:S(2)}, u32[]{:S(2)}) collective-permute-start(bf16[16,4096]{1,0:T(8,128)(2,1)} %get-tuple-element.1244), channel_id=1, source_target_pairs={{0,8},{8,16},{16,24},{1,9},{9,17},{17,25},{2,10},{10,18},{18,26},{... | collective-permute-start | bytes 393224 | tf_op jit(solution)/shard_map/while/body/eval_jaxpr/ppermute | solution.py:14
  233.5 5.3 copy-start.5
  236.0 5.1 copy-start.7
  237.5 3.6 copy-start.14
  241.1 8.9 %collective-permute-start = (bf16[16,4096]{1,0:T(8,128)(2,1)}, bf16[16,4096]{1,0:T(8,128)(2,1)S(1)}, u32[]{:S(2)}, u32[]{:S(2)}) collective-permute-start(bf16[16,4096]{1,0:T(8,128)(2,1)} %get-tuple-element.1244), channel_id=1, source_target_pairs={{0,8},{8,16},{16,24},{1,9},{9,17},{17,25},{2,10},{10,18},{18,26},{... | collective-permute-start | bytes 393224 | tf_op jit(solution)/shard_map/while/body/eval_jaxpr/ppermute | solution.py:14
  253.8 5.3 copy-start.5
  256.3 5.1 copy-start.7
  257.8 3.6 copy-start.14
  261.4 8.8 %collective-permute-start = (bf16[16,4096]{1,0:T(8,128)(2,1)}, bf16[16,4096]{1,0:T(8,128)(2,1)S(1)}, u32[]{:S(2)}, u32[]{:S(2)}) collective-permute-start(bf16[16,4096]{1,0:T(8,128)(2,1)} %get-tuple-element.1244), channel_id=1, source_target_pairs={{0,8},{8,16},{16,24},{1,9},{9,17},{17,25},{2,10},{10,18},{18,26},{... | collective-permute-start | bytes 393224 | tf_op jit(solution)/shard_map/while/body/eval_jaxpr/ppermute | solution.py:14
  275.2 13.9 %collective-permute-start = (bf16[16,4096]{1,0:T(8,128)(2,1)}, bf16[16,4096]{1,0:T(8,128)(2,1)S(1)}, u32[]{:S(2)}, u32[]{:S(2)}) collective-permute-start(bf16[16,4096]{1,0:T(8,128)(2,1)} %get-tuple-element.1244), channel_id=1, source_target_pairs={{0,8},{8,16},{16,24},{1,9},{9,17},{17,25},{2,10},{10,18},{18,26},{... | collective-permute-start | bytes 393224 | tf_op jit(solution)/shard_map/while/body/eval_jaxpr/ppermute | solution.py:14
  294.1 8.8 %collective-permute-start = (bf16[16,4096]{1,0:T(8,128)(2,1)}, bf16[16,4096]{1,0:T(8,128)(2,1)S(1)}, u32[]{:S(2)}, u32[]{:S(2)}) collective-permute-start(bf16[16,4096]{1,0:T(8,128)(2,1)} %get-tuple-element.1244), channel_id=1, source_target_pairs={{0,8},{8,16},{16,24},{1,9},{9,17},{17,25},{2,10},{10,18},{18,26},{... | collective-permute-start | bytes 393224 | tf_op jit(solution)/shard_map/while/body/eval_jaxpr/ppermute | solution.py:14
  308.0 13.4 %collective-permute-start = (bf16[16,4096]{1,0:T(8,128)(2,1)}, bf16[16,4096]{1,0:T(8,128)(2,1)S(1)}, u32[]{:S(2)}, u32[]{:S(2)}) collective-permute-start(bf16[16,4096]{1,0:T(8,128)(2,1)} %get-tuple-element.1244), channel_id=1, source_target_pairs={{0,8},{8,16},{16,24},{1,9},{9,17},{17,25},{2,10},{10,18},{18,26},{... | collective-permute-start | bytes 393224 | tf_op jit(solution)/shard_map/while/body/eval_jaxpr/ppermute | solution.py:14
  326.2 7.4 %collective-permute-start.1 = (bf16[16,4096]{1,0:T(8,128)(2,1)}, bf16[16,4096]{1,0:T(8,128)(2,1)S(1)}, u32[]{:S(2)}, u32[]{:S(2)}) collective-permute-start(bf16[16,4096]{1,0:T(8,128)(2,1)} %get-tuple-element.1274), channel_id=1, source_target_pairs={{8,0},{16,8},{24,16},{9,1},{17,9},{25,17},{10,2},{18,10},{26,18},{... | collective-permute-start | bytes 393224 | tf_op jit(solution)/shard_map/while/body/eval_jaxpr/ppermute | solution.py:14
  335.5 8.7 %collective-permute-start.1 = (bf16[16,4096]{1,0:T(8,128)(2,1)}, bf16[16,4096]{1,0:T(8,128)(2,1)S(1)}, u32[]{:S(2)}, u32[]{:S(2)}) collective-permute-start(bf16[16,4096]{1,0:T(8,128)(2,1)} %get-tuple-element.1274), channel_id=1, source_target_pairs={{8,0},{16,8},{24,16},{9,1},{17,9},{25,17},{10,2},{18,10},{26,18},{... | collective-permute-start | bytes 393224 | tf_op jit(solution)/shard_map/while/body/eval_jaxpr/ppermute | solution.py:14
  346.1 40.6 %collective-permute-start.1 = (bf16[16,4096]{1,0:T(8,128)(2,1)}, bf16[16,4096]{1,0:T(8,128)(2,1)S(1)}, u32[]{:S(2)}, u32[]{:S(2)}) collective-permute-start(bf16[16,4096]{1,0:T(8,128)(2,1)} %get-tuple-element.1274), channel_id=1, source_target_pairs={{8,0},{16,8},{24,16},{9,1},{17,9},{25,17},{10,2},{18,10},{26,18},{... | collective-permute-start | bytes 393224 | tf_op jit(solution)/shard_map/while/body/eval_jaxpr/ppermute | solution.py:14
  389.5 4.5 copy-start.8
  397.1 3.2 copy-start.12
  400.4 8.7 %collective-permute-start.1 = (bf16[16,4096]{1,0:T(8,128)(2,1)}, bf16[16,4096]{1,0:T(8,128)(2,1)S(1)}, u32[]{:S(2)}, u32[]{:S(2)}) collective-permute-start(bf16[16,4096]{1,0:T(8,128)(2,1)} %get-tuple-element.1274), channel_id=1, source_target_pairs={{8,0},{16,8},{24,16},{9,1},{17,9},{25,17},{10,2},{18,10},{26,18},{... | collective-permute-start | bytes 393224 | tf_op jit(solution)/shard_map/while/body/eval_jaxpr/ppermute | solution.py:14
  411.9 4.5 copy-start.8
  422.8 8.7 %collective-permute-start.1 = (bf16[16,4096]{1,0:T(8,128)(2,1)}, bf16[16,4096]{1,0:T(8,128)(2,1)S(1)}, u32[]{:S(2)}, u32[]{:S(2)}) collective-permute-start(bf16[16,4096]{1,0:T(8,128)(2,1)} %get-tuple-element.1274), channel_id=1, source_target_pairs={{8,0},{16,8},{24,16},{9,1},{17,9},{25,17},{10,2},{18,10},{26,18},{... | collective-permute-start | bytes 393224 | tf_op jit(solution)/shard_map/while/body/eval_jaxpr/ppermute | solution.py:14
  434.4 4.4 copy-start.8
  445.3 8.7 %collective-permute-start.1 = (bf16[16,4096]{1,0:T(8,128)(2,1)}, bf16[16,4096]{1,0:T(8,128)(2,1)S(1)}, u32[]{:S(2)}, u32[]{:S(2)}) collective-permute-start(bf16[16,4096]{1,0:T(8,128)(2,1)} %get-tuple-element.1274), channel_id=1, source_target_pairs={{8,0},{16,8},{24,16},{9,1},{17,9},{25,17},{10,2},{18,10},{26,18},{... | collective-permute-start | bytes 393224 | tf_op jit(solution)/shard_map/while/body/eval_jaxpr/ppermute | solution.py:14
  456.8 4.5 copy-start.8
  464.5 3.2 copy-start.12
  467.7 8.7 %collective-permute-start.1 = (bf16[16,4096]{1,0:T(8,128)(2,1)}, bf16[16,4096]{1,0:T(8,128)(2,1)S(1)}, u32[]{:S(2)}, u32[]{:S(2)}) collective-permute-start(bf16[16,4096]{1,0:T(8,128)(2,1)} %get-tuple-element.1274), channel_id=1, source_target_pairs={{8,0},{16,8},{24,16},{9,1},{17,9},{25,17},{10,2},{18,10},{26,18},{... | collective-permute-start | bytes 393224 | tf_op jit(solution)/shard_map/while/body/eval_jaxpr/ppermute | solution.py:14
  479.2 4.5 copy-start.8
  490.1 8.7 %collective-permute-start.1 = (bf16[16,4096]{1,0:T(8,128)(2,1)}, bf16[16,4096]{1,0:T(8,128)(2,1)S(1)}, u32[]{:S(2)}, u32[]{:S(2)}) collective-permute-start(bf16[16,4096]{1,0:T(8,128)(2,1)} %get-tuple-element.1274), channel_id=1, source_target_pairs={{8,0},{16,8},{24,16},{9,1},{17,9},{25,17},{10,2},{18,10},{26,18},{... | collective-permute-start | bytes 393224 | tf_op jit(solution)/shard_map/while/body/eval_jaxpr/ppermute | solution.py:14
  501.7 4.4 copy-start.8
  512.6 8.7 %collective-permute-start.1 = (bf16[16,4096]{1,0:T(8,128)(2,1)}, bf16[16,4096]{1,0:T(8,128)(2,1)S(1)}, u32[]{:S(2)}, u32[]{:S(2)}) collective-permute-start(bf16[16,4096]{1,0:T(8,128)(2,1)} %get-tuple-element.1274), channel_id=1, source_target_pairs={{8,0},{16,8},{24,16},{9,1},{17,9},{25,17},{10,2},{18,10},{26,18},{... | collective-permute-start | bytes 393224 | tf_op jit(solution)/shard_map/while/body/eval_jaxpr/ppermute | solution.py:14
  524.1 4.5 copy-start.8
  535.0 8.7 %collective-permute-start.1 = (bf16[16,4096]{1,0:T(8,128)(2,1)}, bf16[16,4096]{1,0:T(8,128)(2,1)S(1)}, u32[]{:S(2)}, u32[]{:S(2)}) collective-permute-start(bf16[16,4096]{1,0:T(8,128)(2,1)} %get-tuple-element.1274), channel_id=1, source_target_pairs={{8,0},{16,8},{24,16},{9,1},{17,9},{25,17},{10,2},{18,10},{26,18},{... | collective-permute-start | bytes 393224 | tf_op jit(solution)/shard_map/while/body/eval_jaxpr/ppermute | solution.py:14
  546.5 4.5 copy-start.8
  557.4 8.1 %collective-permute-start.1 = (bf16[16,4096]{1,0:T(8,128)(2,1)}, bf16[16,4096]{1,0:T(8,128)(2,1)S(1)}, u32[]{:S(2)}, u32[]{:S(2)}) collective-permute-start(bf16[16,4096]{1,0:T(8,128)(2,1)} %get-tuple-element.1274), channel_id=1, source_target_pairs={{8,0},{16,8},{24,16},{9,1},{17,9},{25,17},{10,2},{18,10},{26,18},{... | collective-permute-start | bytes 393224 | tf_op jit(solution)/shard_map/while/body/eval_jaxpr/ppermute | solution.py:14
  (50 other events, 130.7 us)
Sparse Core Ops, SparseCore 0:
  9.6 25.0 all-gather.8
  36.2 21.8 all-gather.10
  59.7 21.8 all-gather.12
  83.1 21.8 all-gather.14
  576.1 95.7 all-reduce.2
where the time goes:
time: 691 us; the launch traced here: 682 us
  waiting for transfers between devices  231 us (33%)
  matrix products  135 us (20%)
  local copies, waits for them, and re-layouts  130 us (19%)
  other arithmetic  124 us (18%)
  starting transfers between devices  47.5 us (7%)
  between operations  13.8 us (2%)
    psum x1, waiting for transfers between devices, on_device(): lax.psum(full_q.astype(jnp.bfloat16), 'rep').astype(jnp.float32)  96 us
    dynamic_slice x110, local copies, waits for them, and re-layouts, store_slot(): old_value = lax.dynamic_index_in_dim(store, slot_at, 0, keepdims=False)  89.3 us
    dynamic_update_slice x77, other arithmetic, store_slot(): return lax.dynamic_update_index_in_dim(store, fresh, slot_at, 0)  83.6 us
    ppermute x22, starting transfers between devices, from_behind(): return lax.ppermute(block, axis, route)  47.3 us
    ppermute x22, waiting for transfers between devices, from_behind(): return lax.ppermute(block, axis, route)  38.9 us
    all_gather x1, waiting for transfers between devices, on_device(): lax.all_gather(w_v[0], 'rep', axis=0, tiled=True)  23.5 us
    all_gather x1, waiting for transfers between devices, on_device(): lax.all_gather(w_k[0], 'rep', axis=0, tiled=True)  23.5 us
    all_gather x1, waiting for transfers between devices, on_device(): lax.all_gather(w_out[0], 'rep', axis=0, tiled=True)  23.3 us
  transfers between devices with their start and end apart: 27, of which 14 were waited for; matrix products, arithmetic and copies ran while one was open for 21% of the time, Pallas kernels for 0%

commit v1 on v0

--- a/solution.py
+++ b/solution.py
@@ -2,6 +2,7 @@
 import jax.numpy as jnp
 from jax import lax
 from jax.sharding import PartitionSpec as P
+from jax.lax import all_gather
 
 MB = 8
 ROWS = 16
@@ -197,8 +198,9 @@
     full_v = local_grad(saved_normed, saved_dv)
     full_o = local_grad(saved_rows, saved_heads)
     share_width = width // rep_count
+    _read_joints = lambda point, mesh_dim: jnp.sum(all_gather(point, mesh_dim), 0)
     totals = (
-        lax.psum(full_q.astype(jnp.bfloat16), "rep").astype(jnp.float32),
+        _read_joints(full_q.astype(jnp.bfloat16), "rep").astype(jnp.float32),
         lax.psum(full_k.astype(jnp.bfloat16), "rep").astype(jnp.float32),
         lax.psum(full_v.astype(jnp.bfloat16), "rep").astype(jnp.float32),
         lax.psum(full_o.astype(jnp.bfloat16), "rep").astype(jnp.float32),

time: 691 us -> 790 us (1.14)
  waiting for transfers between devices: 231 us -> 297 us
  matrix products: 135 us -> 165 us
  local copies, waits for them, and re-layouts: 130 us -> 121 us
    all_gather x0 -> x1, waiting for transfers between devices: none -> 80.1 us  [on_device(): all_gather(point, mesh_dim)]
    psum x1, waiting for transfers between devices: 96 us -> 73.4 us  [on_device(): lax.psum(full_k.astype(jnp.bfloat16), 'rep').astype(jnp.float32)]
    dot_general x8, matrix products: 1.99 us -> 14 us  [forward_layer(): jnp.dot(normed, weight_k, preferred_element_type=jnp.float32)]
    dynamic_slice x110, local copies, waits for them, and re-layouts: 89.3 us -> 79.5 us  [store_slot(): old_value = lax.dynamic_index_in_dim(store, slot_at, 0, keepdims=False)]
    ppermute x22, waiting for transfers between devices: 38.9 us -> 47.3 us  [from_behind(): return lax.ppermute(block, axis, route)]
  transfers between devices with their start and end apart: 27 -> 28, of which waited for: 14 -> 16; matrix products, arithmetic and copies ran while one was open for 21% -> 18% of each run, Pallas kernels for 0% -> 0%
where the time goes in v1:
time: 790 us; the launch traced here: 781 us
  waiting for transfers between devices  297 us (38%)
  matrix products  165 us (21%)
  other arithmetic  130 us (16%)
  local copies, waits for them, and re-layouts  121 us (15%)
  starting transfers between devices  53.1 us (7%)
  between operations  14.2 us (2%)
    dynamic_update_slice x77, other arithmetic, store_slot(): return lax.dynamic_update_index_in_dim(store, fresh, slot_at, 0)  83.7 us
    all_gather x1, waiting for transfers between devices, on_device(): all_gather(point, mesh_dim)  80.1 us
    dynamic_slice x110, local copies, waits for them, and re-layouts, store_slot(): old_value = lax.dynamic_index_in_dim(store, slot_at, 0, keepdims=False)  79.5 us
    psum x1, waiting for transfers between devices, on_device(): lax.psum(full_k.astype(jnp.bfloat16), 'rep').astype(jnp.float32)  73.4 us
    ppermute x22, starting transfers between devices, from_behind(): return lax.ppermute(block, axis, route)  52.8 us
    ppermute x22, waiting for transfers between devices, from_behind(): return lax.ppermute(block, axis, route)  47.3 us
    all_gather x1, waiting for transfers between devices, on_device(): lax.all_gather(w_v[0], 'rep', axis=0, tiled=True)  23.5 us
    all_gather x1, waiting for transfers between devices, on_device(): lax.all_gather(w_k[0], 'rep', axis=0, tiled=True)  23.5 us
  transfers between devices with their start and end apart: 28, of which 16 were waited for; matrix products, arithmetic and copies ran while one was open for 18% of the time, Pallas kernels for 0%

profile of v1, /device:TPU:0, one launch (start us, length us, event | category | flops | bytes accessed | tf_op | source)
XLA Modules:
  0.0 780.9 jit_solution(3889571451791571729)
XLA Ops:
  11.5 23.2 %all-gather.11.cloned.1.call-done = bf16[1,4096,128]{2,1,0:T(8,128)(2,1)} async-done(((bf16[1,512,128]{2,1,0:T(8,128)(2,1)}), bf16[1,4096,128]{2,1,0:T(8,128)(2,1)}) %all-gather.11.cloned.1.call-update) | async-done | bytes 1048592 | tf_op jit(solution)/shard_map/all_gather | solution.py:111
  34.6 23.5 %all-gather.13.cloned.1.call-done = bf16[1,4096,128]{2,1,0:T(8,128)(2,1)} async-done(((bf16[1,512,128]{2,1,0:T(8,128)(2,1)}), bf16[1,4096,128]{2,1,0:T(8,128)(2,1)}) %all-gather.13.cloned.1.call-update) | async-done | bytes 1048592 | tf_op jit(solution)/shard_map/all_gather | solution.py:112
  58.1 23.5 %all-gather.15.cloned.1.call-done = bf16[1,4096,128]{2,1,0:T(8,128)(2,1)} async-done(((bf16[1,512,128]{2,1,0:T(8,128)(2,1)}), bf16[1,4096,128]{2,1,0:T(8,128)(2,1)}) %all-gather.15.cloned.1.call-update) | async-done | bytes 1048592 | tf_op jit(solution)/shard_map/all_gather | solution.py:113
  81.6 23.3 %all-gather.17.cloned.1.call-done = bf16[1,4096,128]{2,1,0:T(8,128)(2,1)} async-done(((bf16[1,512,128]{2,1,0:T(8,128)(2,1)}), bf16[1,4096,128]{2,1,0:T(8,128)(2,1)}) %all-gather.17.cloned.1.call-update) | async-done | bytes 1048592 | tf_op jit(solution)/shard_map/all_gather | solution.py:114
  108.6 244.8 %while.49 = (s32[]{:T(128)}, bf16[16,4096]{1,0:T(8,128)(2,1)S(1)}, bf16[8,16,4096]{2,1,0:T(8,128)(2,1)}, bf16[8,16,4096]{2,1,0:T(8,128)(2,1)S(1)}, bf16[8,16,128...) while((s32[]{:T(128)}, bf16[16,4096]{1,0:T(8,128)(2,1)S(1)}, ...), condition=%wide.region_7.8_spmd, body=%wide.region_2.7_spmd.sunk | while | flops 68175368 | bytes 15864699 | solution.py:160
  111.1 12.2 %conditional.4 = (bf16[16,4096]{1,0:T(8,128)(2,1)S(1)}, bf16[16,4096]{1,0:T(8,128)(2,1)}, bf16[16,128]{1,0:T(8,128)(2,1)}, bf16[16,128]{1,0:T(8,128)(2,1)}, bf16...) conditional(s32[]{:T(128)} %convert_element_type.176, () %tuple.108, (bf16[16,4096]{1,0:T(8,128)(2,1)S(1)}, ...), branch_computations={%region_3.3_spmd, %region_4.6_spmd} | conditional | flops 67970560 | bytes 13683192 | solution.py:141
  112.9 1.8 convolution_convert_fusion.2
  114.7 1.7 convolution_convert_fusion.3
  117.2 1.8 convolution_convert_fusion.1
  134.1 12.2 %conditional.4 = (bf16[16,4096]{1,0:T(8,128)(2,1)S(1)}, bf16[16,4096]{1,0:T(8,128)(2,1)}, bf16[16,128]{1,0:T(8,128)(2,1)}, bf16[16,128]{1,0:T(8,128)(2,1)}, bf16...) conditional(s32[]{:T(128)} %convert_element_type.176, () %tuple.108, (bf16[16,4096]{1,0:T(8,128)(2,1)S(1)}, ...), branch_computations={%region_3.3_spmd, %region_4.6_spmd} | conditional | flops 67970560 | bytes 13683192 | solution.py:141
  135.9 1.8 convolution_convert_fusion.2
  140.2 1.8 convolution_convert_fusion.1
  157.1 12.2 %conditional.4 = (bf16[16,4096]{1,0:T(8,128)(2,1)S(1)}, bf16[16,4096]{1,0:T(8,128)(2,1)}, bf16[16,128]{1,0:T(8,128)(2,1)}, bf16[16,128]{1,0:T(8,128)(2,1)}, bf16...) conditional(s32[]{:T(128)} %convert_element_type.176, () %tuple.108, (bf16[16,4096]{1,0:T(8,128)(2,1)S(1)}, ...), branch_computations={%region_3.3_spmd, %region_4.6_spmd} | conditional | flops 67970560 | bytes 13683192 | solution.py:141
  158.9 1.8 convolution_convert_fusion.2
  160.6 1.7 convolution_convert_fusion.3
  163.2 1.8 convolution_convert_fusion.1
  180.3 12.2 %conditional.4 = (bf16[16,4096]{1,0:T(8,128)(2,1)S(1)}, bf16[16,4096]{1,0:T(8,128)(2,1)}, bf16[16,128]{1,0:T(8,128)(2,1)}, bf16[16,128]{1,0:T(8,128)(2,1)}, bf16...) conditional(s32[]{:T(128)} %convert_element_type.176, () %tuple.108, (bf16[16,4096]{1,0:T(8,128)(2,1)S(1)}, ...), branch_computations={%region_3.3_spmd, %region_4.6_spmd} | conditional | flops 67970560 | bytes 13683192 | solution.py:141
  182.0 1.8 convolution_convert_fusion.2
  183.8 1.7 convolution_convert_fusion.3
  186.3 1.8 convolution_convert_fusion.1
  192.5 1.9 collective-permute-start
  203.8 12.2 %conditional.4 = (bf16[16,4096]{1,0:T(8,128)(2,1)S(1)}, bf16[16,4096]{1,0:T(8,128)(2,1)}, bf16[16,128]{1,0:T(8,128)(2,1)}, bf16[16,128]{1,0:T(8,128)(2,1)}, bf16...) conditional(s32[]{:T(128)} %convert_element_type.176, () %tuple.108, (bf16[16,4096]{1,0:T(8,128)(2,1)S(1)}, ...), branch_computations={%region_3.3_spmd, %region_4.6_spmd} | conditional | flops 67970560 | bytes 13683192 | solution.py:141
  205.6 1.8 convolution_convert_fusion.2
  207.4 1.7 convolution_convert_fusion.3
  209.9 1.8 convolution_convert_fusion.1
  216.1 1.9 collective-permute-start
  227.5 12.2 %conditional.4 = (bf16[16,4096]{1,0:T(8,128)(2,1)S(1)}, bf16[16,4096]{1,0:T(8,128)(2,1)}, bf16[16,128]{1,0:T(8,128)(2,1)}, bf16[16,128]{1,0:T(8,128)(2,1)}, bf16...) conditional(s32[]{:T(128)} %convert_element_type.176, () %tuple.108, (bf16[16,4096]{1,0:T(8,128)(2,1)S(1)}, ...), branch_computations={%region_3.3_spmd, %region_4.6_spmd} | conditional | flops 67970560 | bytes 13683192 | solution.py:141
  229.2 1.8 convolution_convert_fusion.2
  233.5 1.8 convolution_convert_fusion.1
  239.7 1.9 collective-permute-start
  251.0 12.2 %conditional.4 = (bf16[16,4096]{1,0:T(8,128)(2,1)S(1)}, bf16[16,4096]{1,0:T(8,128)(2,1)}, bf16[16,128]{1,0:T(8,128)(2,1)}, bf16[16,128]{1,0:T(8,128)(2,1)}, bf16...) conditional(s32[]{:T(128)} %convert_element_type.176, () %tuple.108, (bf16[16,4096]{1,0:T(8,128)(2,1)S(1)}, ...), branch_computations={%region_3.3_spmd, %region_4.6_spmd} | conditional | flops 67970560 | bytes 13683192 | solution.py:141
  252.8 1.8 convolution_convert_fusion.2
  257.1 1.8 convolution_convert_fusion.1
  263.2 1.9 collective-permute-start
  274.6 12.2 %conditional.4 = (bf16[16,4096]{1,0:T(8,128)(2,1)S(1)}, bf16[16,4096]{1,0:T(8,128)(2,1)}, bf16[16,128]{1,0:T(8,128)(2,1)}, bf16[16,128]{1,0:T(8,128)(2,1)}, bf16...) conditional(s32[]{:T(128)} %convert_element_type.176, () %tuple.108, (bf16[16,4096]{1,0:T(8,128)(2,1)S(1)}, ...), branch_computations={%region_3.3_spmd, %region_4.6_spmd} | conditional | flops 67970560 | bytes 13683192 | solution.py:141
  276.4 1.8 convolution_convert_fusion.2
  280.7 1.8 convolution_convert_fusion.1
  286.9 1.9 collective-permute-start
  298.3 3.0 conditional.4
  301.3 11.1 %collective-permute-start = (bf16[16,4096]{1,0:T(8,128)(2,1)S(1)}, bf16[16,4096]{1,0:T(8,128)(2,1)S(1)}, u32[]{:S(2)}, u32[]{:S(2)}) collective-permute-start(bf16[16,4096]{1,0:T(8,128)(2,1)S(1)} %get-tuple-element.1241), channel_id=1, source_target_pairs={{0,8},{8,16},{16,24},{1,9},{9,17},{17,25},{2,10},{10,18},{18,26},{... | collective-permute-start | bytes 393224 | tf_op jit(solution)/shard_map/while/body/eval_jaxpr/ppermute | solution.py:15
  320.3 3.0 conditional.4
  323.3 3.5 collective-permute-start
  334.7 3.0 conditional.4
  337.8 10.4 %collective-permute-start = (bf16[16,4096]{1,0:T(8,128)(2,1)S(1)}, bf16[16,4096]{1,0:T(8,128)(2,1)S(1)}, u32[]{:S(2)}, u32[]{:S(2)}) collective-permute-start(bf16[16,4096]{1,0:T(8,128)(2,1)S(1)} %get-tuple-element.1241), channel_id=1, source_target_pairs={{0,8},{8,16},{16,24},{1,9},{9,17},{17,25},{2,10},{10,18},{18,26},{... | collective-permute-start | bytes 393224 | tf_op jit(solution)/shard_map/while/body/eval_jaxpr/ppermute | solution.py:15
  356.5 245.9 %while.50 = (s32[]{:T(128)}, bf16[16,4096]{1,0:T(8,128)(2,1)S(1)}, bf16[8,16,4096]{2,1,0:T(8,128)(2,1)}, bf16[8,16,128]{2,1,0:T(8,128)(2,1)}, bf16[8,16,128]{2,1...) while((s32[]{:T(128)}, bf16[16,4096]{1,0:T(8,128)(2,1)S(1)}, ...), condition=%wide.region_15.16_spmd, body=%wide.region_8.15_spmd.sunk | while | flops 68961784 | bytes 13517776 | solution.py:193
  356.5 1.8 conditional.5
  365.2 1.8 conditional.5
  373.1 5.5 collective-permute-done.1
  378.6 1.8 conditional.5
  386.5 36.7 %collective-permute-done.1 = bf16[16,4096]{1,0:T(8,128)(2,1)S(1)} collective-permute-done((bf16[16,4096]{1,0:T(8,128)(2,1)S(1)}, bf16[16,4096]{1,0:T(8,128)(2,1)S(1)}, u32[]{:S(2)}, u32[]{:S(2)}) %collective-permute-start.1) | collective-permute-done | bytes 131104 | tf_op jit(solution)/shard_map/while/body/eval_jaxpr/ppermute | solution.py:15
  423.2 14.3 %conditional.5 = (bf16[16,4096]{1,0:T(8,128)(2,1)S(1)}, bf16[16,4096]{1,0:T(8,128)(2,1)S(1)}, bf16[16,128]{1,0:T(8,128)(2,1)}, bf16[16,128]{1,0:T(8,128)(2,1)}, bf16[16,128]{1,0:T(8,128)(2,1)}) conditional(s32[]{:T(128)} %convert_element_type.177, () %tuple.112, (pred[]{:T(512)}, bf16[8,16,4096]{2,1,0:T(8,128)(2,1)}, s32[]{:T(128)}, ...), branch_computations={%region_9.9_spmd, %region_10.14_spmd} | conditional | flops 68890096 | bytes 12274714 | solution.py:176
  445.7 14.3 %conditional.5 = (bf16[16,4096]{1,0:T(8,128)(2,1)S(1)}, bf16[16,4096]{1,0:T(8,128)(2,1)S(1)}, bf16[16,128]{1,0:T(8,128)(2,1)}, bf16[16,128]{1,0:T(8,128)(2,1)}, bf16[16,128]{1,0:T(8,128)(2,1)}) conditional(s32[]{:T(128)} %convert_element_type.177, () %tuple.112, (pred[]{:T(512)}, bf16[8,16,4096]{2,1,0:T(8,128)(2,1)}, s32[]{:T(128)}, ...), branch_computations={%region_9.9_spmd, %region_10.14_spmd} | conditional | flops 68890096 | bytes 12274714 | solution.py:176
  468.2 14.3 %conditional.5 = (bf16[16,4096]{1,0:T(8,128)(2,1)S(1)}, bf16[16,4096]{1,0:T(8,128)(2,1)S(1)}, bf16[16,128]{1,0:T(8,128)(2,1)}, bf16[16,128]{1,0:T(8,128)(2,1)}, bf16[16,128]{1,0:T(8,128)(2,1)}) conditional(s32[]{:T(128)} %convert_element_type.177, () %tuple.112, (pred[]{:T(512)}, bf16[8,16,4096]{2,1,0:T(8,128)(2,1)}, s32[]{:T(128)}, ...), branch_computations={%region_9.9_spmd, %region_10.14_spmd} | conditional | flops 68890096 | bytes 12274714 | solution.py:176
  490.6 14.3 %conditional.5 = (bf16[16,4096]{1,0:T(8,128)(2,1)S(1)}, bf16[16,4096]{1,0:T(8,128)(2,1)S(1)}, bf16[16,128]{1,0:T(8,128)(2,1)}, bf16[16,128]{1,0:T(8,128)(2,1)}, bf16[16,128]{1,0:T(8,128)(2,1)}) conditional(s32[]{:T(128)} %convert_element_type.177, () %tuple.112, (pred[]{:T(512)}, bf16[8,16,4096]{2,1,0:T(8,128)(2,1)}, s32[]{:T(128)}, ...), branch_computations={%region_9.9_spmd, %region_10.14_spmd} | conditional | flops 68890096 | bytes 12274714 | solution.py:176
  513.1 14.3 %conditional.5 = (bf16[16,4096]{1,0:T(8,128)(2,1)S(1)}, bf16[16,4096]{1,0:T(8,128)(2,1)S(1)}, bf16[16,128]{1,0:T(8,128)(2,1)}, bf16[16,128]{1,0:T(8,128)(2,1)}, bf16[16,128]{1,0:T(8,128)(2,1)}) conditional(s32[]{:T(128)} %convert_element_type.177, () %tuple.112, (pred[]{:T(512)}, bf16[8,16,4096]{2,1,0:T(8,128)(2,1)}, s32[]{:T(128)}, ...), branch_computations={%region_9.9_spmd, %region_10.14_spmd} | conditional | flops 68890096 | bytes 12274714 | solution.py:176
  535.6 14.3 %conditional.5 = (bf16[16,4096]{1,0:T(8,128)(2,1)S(1)}, bf16[16,4096]{1,0:T(8,128)(2,1)S(1)}, bf16[16,128]{1,0:T(8,128)(2,1)}, bf16[16,128]{1,0:T(8,128)(2,1)}, bf16[16,128]{1,0:T(8,128)(2,1)}) conditional(s32[]{:T(128)} %convert_element_type.177, () %tuple.112, (pred[]{:T(512)}, bf16[8,16,4096]{2,1,0:T(8,128)(2,1)}, s32[]{:T(128)}, ...), branch_computations={%region_9.9_spmd, %region_10.14_spmd} | conditional | flops 68890096 | bytes 12274714 | solution.py:176
  558.1 14.3 %conditional.5 = (bf16[16,4096]{1,0:T(8,128)(2,1)S(1)}, bf16[16,4096]{1,0:T(8,128)(2,1)S(1)}, bf16[16,128]{1,0:T(8,128)(2,1)}, bf16[16,128]{1,0:T(8,128)(2,1)}, bf16[16,128]{1,0:T(8,128)(2,1)}) conditional(s32[]{:T(128)} %convert_element_type.177, () %tuple.112, (pred[]{:T(512)}, bf16[8,16,4096]{2,1,0:T(8,128)(2,1)}, s32[]{:T(128)}, ...), branch_computations={%region_9.9_spmd, %region_10.14_spmd} | conditional | flops 68890096 | bytes 12274714 | solution.py:176
  580.6 14.3 %conditional.5 = (bf16[16,4096]{1,0:T(8,128)(2,1)S(1)}, bf16[16,4096]{1,0:T(8,128)(2,1)S(1)}, bf16[16,128]{1,0:T(8,128)(2,1)}, bf16[16,128]{1,0:T(8,128)(2,1)}, bf16[16,128]{1,0:T(8,128)(2,1)}) conditional(s32[]{:T(128)} %convert_element_type.177, () %tuple.112, (pred[]{:T(512)}, bf16[8,16,4096]{2,1,0:T(8,128)(2,1)}, s32[]{:T(128)}, ...), branch_computations={%region_9.9_spmd, %region_10.14_spmd} | conditional | flops 68890096 | bytes 12274714 | solution.py:176
  602.4 2.9 fusion.37
  606.7 2.2 fusion.38
  611.2 73.4 %all-reduce.3.cloned.1.call-done = (bf16[4096,128]{1,0:T(8,128)(2,1)}, bf16[4096,128]{1,0:T(8,128)(2,1)}, bf16[4096,128]{1,0:T(8,128)(2,1)}) async-done(((bf16[4096,128]{1,0:T(8,128)(2,1)}, bf16[4096,128]{1,0:T(8,128)(2,1)}, bf16[4096,128]{1,0:T(8,128)(2,1)}), (bf16[4096,128]{1,0:T(8,128)(2,1)}, bf16[4096,128]{1,0:T(8,128)(2,1)}, bf16[4096,128]{1,0:T(8,128)(2,1)})) %all-reduce.3.cloned.1.call-update) | async-done | bytes 3145744 | tf_op jit(solution)/shard_map/psum | solution.py:204
  686.2 1.8 convert_bitcast_fusion
  688.0 80.1 %all-gather.19.cloned.1.call-done = bf16[32768,128]{1,0:T(8,128)(2,1)} async-done(((bf16[4096,128]{1,0:T(8,128)(2,1)}), bf16[32768,128]{1,0:T(8,128)(2,1)}) %all-gather.19.cloned.1.call-update) | async-done | bytes 8388624 | tf_op jit(solution)/shard_map/all_gather | solution.py:201
  768.1 5.2 reduce_sum.84
  (556 shorter events, 395.0 us)
Async XLA Ops:
  7.2 3.6 copy-start
  7.2 27.5 %all-gather.11.cloned.1.call-start = ((), (), s32[]{:S(2)}) async-start(), calls=%async_computation | async-start | bytes 1179648 | tf_op jit(solution)/shard_map/all_gather | solution.py:111
  7.9 50.2 %all-gather.13.cloned.1.call-start = ((), (), s32[]{:S(2)}) async-start(), calls=%async_computation.1 | async-start | bytes 1179648 | tf_op jit(solution)/shard_map/all_gather | solution.py:112
  8.7 72.9 %all-gather.15.cloned.1.call-start = ((), (), s32[]{:S(2)}) async-start(), calls=%async_computation.2 | async-start | bytes 1179648 | tf_op jit(solution)/shard_map/all_gather | solution.py:113
  9.4 95.5 %all-gather.17.cloned.1.call-start = ((), (), s32[]{:S(2)}) async-start(), calls=%async_computation.3 | async-start | bytes 1179648 | tf_op jit(solution)/shard_map/all_gather | solution.py:114
  10.0 674.6 %all-reduce.3.cloned.1.call-start = ((), (), s32[]{:S(2)}) async-start(), calls=%async_computation.5 | async-start | bytes 6291456 | tf_op jit(solution)/shard_map/psum | solution.py:204
  34.6 74.0 %copy-start.1 = (bf16[1,4096,128]{2,1,0:T(8,128)(2,1)S(1)}, bf16[1,4096,128]{2,1,0:T(8,128)(2,1)}, u32[]{:S(2)}) copy-start(bf16[1,4096,128]{2,1,0:T(8,128)(2,1)} %all-gather.11.cloned.1.call-done) | copy-start | bytes 3145732
  58.1 50.5 %copy-start.2 = (bf16[1,4096,128]{2,1,0:T(8,128)(2,1)S(1)}, bf16[1,4096,128]{2,1,0:T(8,128)(2,1)}, u32[]{:S(2)}) copy-start(bf16[1,4096,128]{2,1,0:T(8,128)(2,1)} %all-gather.13.cloned.1.call-done) | copy-start | bytes 3145732
  111.2 6.1 copy-start.3
  111.2 10.5 %copy-start.5 = (bf16[4096,128]{1,0:T(8,128)(2,1)S(1)}, bf16[4096,128]{1,0:T(8,128)(2,1)}, u32[]{:S(2)}) copy-start(bf16[4096,128]{1,0:T(8,128)(2,1)} %get-tuple-element.838) | copy-start | bytes 3145732 | tf_op jit(solution)/shard_map/while/body/eval_jaxpr/cond
  123.4 8.2 %collective-permute-start = (bf16[16,4096]{1,0:T(8,128)(2,1)S(1)}, bf16[16,4096]{1,0:T(8,128)(2,1)S(1)}, u32[]{:S(2)}, u32[]{:S(2)}) collective-permute-start(bf16[16,4096]{1,0:T(8,128)(2,1)S(1)} %get-tuple-element.1241), channel_id=1, source_target_pairs={{0,8},{8,16},{16,24},{1,9},{9,17},{17,25},{2,10},{10,18},{18,26},{... | collective-permute-start | bytes 393224 | tf_op jit(solution)/shard_map/while/body/eval_jaxpr/ppermute | solution.py:15
  134.1 6.1 copy-start.3
  134.1 10.5 %copy-start.5 = (bf16[4096,128]{1,0:T(8,128)(2,1)S(1)}, bf16[4096,128]{1,0:T(8,128)(2,1)}, u32[]{:S(2)}) copy-start(bf16[4096,128]{1,0:T(8,128)(2,1)} %get-tuple-element.838) | copy-start | bytes 3145732 | tf_op jit(solution)/shard_map/while/body/eval_jaxpr/cond
  146.3 8.2 %collective-permute-start = (bf16[16,4096]{1,0:T(8,128)(2,1)S(1)}, bf16[16,4096]{1,0:T(8,128)(2,1)S(1)}, u32[]{:S(2)}, u32[]{:S(2)}) collective-permute-start(bf16[16,4096]{1,0:T(8,128)(2,1)S(1)} %get-tuple-element.1241), channel_id=1, source_target_pairs={{0,8},{8,16},{16,24},{1,9},{9,17},{17,25},{2,10},{10,18},{18,26},{... | collective-permute-start | bytes 393224 | tf_op jit(solution)/shard_map/while/body/eval_jaxpr/ppermute | solution.py:15
  157.1 6.1 copy-start.3
  157.1 10.5 %copy-start.5 = (bf16[4096,128]{1,0:T(8,128)(2,1)S(1)}, bf16[4096,128]{1,0:T(8,128)(2,1)}, u32[]{:S(2)}) copy-start(bf16[4096,128]{1,0:T(8,128)(2,1)} %get-tuple-element.838) | copy-start | bytes 3145732 | tf_op jit(solution)/shard_map/while/body/eval_jaxpr/cond
  169.3 8.4 %collective-permute-start = (bf16[16,4096]{1,0:T(8,128)(2,1)S(1)}, bf16[16,4096]{1,0:T(8,128)(2,1)S(1)}, u32[]{:S(2)}, u32[]{:S(2)}) collective-permute-start(bf16[16,4096]{1,0:T(8,128)(2,1)S(1)} %get-tuple-element.1241), channel_id=1, source_target_pairs={{0,8},{8,16},{16,24},{1,9},{9,17},{17,25},{2,10},{10,18},{18,26},{... | collective-permute-start | bytes 393224 | tf_op jit(solution)/shard_map/while/body/eval_jaxpr/ppermute | solution.py:15
  180.3 6.1 copy-start.3
  180.3 10.5 %copy-start.5 = (bf16[4096,128]{1,0:T(8,128)(2,1)S(1)}, bf16[4096,128]{1,0:T(8,128)(2,1)}, u32[]{:S(2)}) copy-start(bf16[4096,128]{1,0:T(8,128)(2,1)} %get-tuple-element.838) | copy-start | bytes 3145732 | tf_op jit(solution)/shard_map/while/body/eval_jaxpr/cond
  192.5 8.8 %collective-permute-start = (bf16[16,4096]{1,0:T(8,128)(2,1)S(1)}, bf16[16,4096]{1,0:T(8,128)(2,1)S(1)}, u32[]{:S(2)}, u32[]{:S(2)}) collective-permute-start(bf16[16,4096]{1,0:T(8,128)(2,1)S(1)} %get-tuple-element.1241), channel_id=1, source_target_pairs={{0,8},{8,16},{16,24},{1,9},{9,17},{17,25},{2,10},{10,18},{18,26},{... | collective-permute-start | bytes 393224 | tf_op jit(solution)/shard_map/while/body/eval_jaxpr/ppermute | solution.py:15
  203.9 6.1 copy-start.3
  203.9 10.5 %copy-start.5 = (bf16[4096,128]{1,0:T(8,128)(2,1)S(1)}, bf16[4096,128]{1,0:T(8,128)(2,1)}, u32[]{:S(2)}) copy-start(bf16[4096,128]{1,0:T(8,128)(2,1)} %get-tuple-element.838) | copy-start | bytes 3145732 | tf_op jit(solution)/shard_map/while/body/eval_jaxpr/cond
  216.1 8.9 %collective-permute-start = (bf16[16,4096]{1,0:T(8,128)(2,1)S(1)}, bf16[16,4096]{1,0:T(8,128)(2,1)S(1)}, u32[]{:S(2)}, u32[]{:S(2)}) collective-permute-start(bf16[16,4096]{1,0:T(8,128)(2,1)S(1)} %get-tuple-element.1241), channel_id=1, source_target_pairs={{0,8},{8,16},{16,24},{1,9},{9,17},{17,25},{2,10},{10,18},{18,26},{... | collective-permute-start | bytes 393224 | tf_op jit(solution)/shard_map/while/body/eval_jaxpr/ppermute | solution.py:15
  227.5 6.1 copy-start.3
  227.5 10.5 %copy-start.5 = (bf16[4096,128]{1,0:T(8,128)(2,1)S(1)}, bf16[4096,128]{1,0:T(8,128)(2,1)}, u32[]{:S(2)}) copy-start(bf16[4096,128]{1,0:T(8,128)(2,1)} %get-tuple-element.838) | copy-start | bytes 3145732 | tf_op jit(solution)/shard_map/while/body/eval_jaxpr/cond
  239.7 8.8 %collective-permute-start = (bf16[16,4096]{1,0:T(8,128)(2,1)S(1)}, bf16[16,4096]{1,0:T(8,128)(2,1)S(1)}, u32[]{:S(2)}, u32[]{:S(2)}) collective-permute-start(bf16[16,4096]{1,0:T(8,128)(2,1)S(1)} %get-tuple-element.1241), channel_id=1, source_target_pairs={{0,8},{8,16},{16,24},{1,9},{9,17},{17,25},{2,10},{10,18},{18,26},{... | collective-permute-start | bytes 393224 | tf_op jit(solution)/shard_map/while/body/eval_jaxpr/ppermute | solution.py:15
  251.0 6.1 copy-start.3
  251.0 10.5 %copy-start.5 = (bf16[4096,128]{1,0:T(8,128)(2,1)S(1)}, bf16[4096,128]{1,0:T(8,128)(2,1)}, u32[]{:S(2)}) copy-start(bf16[4096,128]{1,0:T(8,128)(2,1)} %get-tuple-element.838) | copy-start | bytes 3145732 | tf_op jit(solution)/shard_map/while/body/eval_jaxpr/cond
  263.2 8.9 %collective-permute-start = (bf16[16,4096]{1,0:T(8,128)(2,1)S(1)}, bf16[16,4096]{1,0:T(8,128)(2,1)S(1)}, u32[]{:S(2)}, u32[]{:S(2)}) collective-permute-start(bf16[16,4096]{1,0:T(8,128)(2,1)S(1)} %get-tuple-element.1241), channel_id=1, source_target_pairs={{0,8},{8,16},{16,24},{1,9},{9,17},{17,25},{2,10},{10,18},{18,26},{... | collective-permute-start | bytes 393224 | tf_op jit(solution)/shard_map/while/body/eval_jaxpr/ppermute | solution.py:15
  274.6 6.1 copy-start.3
  274.7 10.5 %copy-start.5 = (bf16[4096,128]{1,0:T(8,128)(2,1)S(1)}, bf16[4096,128]{1,0:T(8,128)(2,1)}, u32[]{:S(2)}) copy-start(bf16[4096,128]{1,0:T(8,128)(2,1)} %get-tuple-element.838) | copy-start | bytes 3145732 | tf_op jit(solution)/shard_map/while/body/eval_jaxpr/cond
  286.9 8.9 %collective-permute-start = (bf16[16,4096]{1,0:T(8,128)(2,1)S(1)}, bf16[16,4096]{1,0:T(8,128)(2,1)S(1)}, u32[]{:S(2)}, u32[]{:S(2)}) collective-permute-start(bf16[16,4096]{1,0:T(8,128)(2,1)S(1)} %get-tuple-element.1241), channel_id=1, source_target_pairs={{0,8},{8,16},{16,24},{1,9},{9,17},{17,25},{2,10},{10,18},{18,26},{... | collective-permute-start | bytes 393224 | tf_op jit(solution)/shard_map/while/body/eval_jaxpr/ppermute | solution.py:15
  301.3 16.4 %collective-permute-start = (bf16[16,4096]{1,0:T(8,128)(2,1)S(1)}, bf16[16,4096]{1,0:T(8,128)(2,1)S(1)}, u32[]{:S(2)}, u32[]{:S(2)}) collective-permute-start(bf16[16,4096]{1,0:T(8,128)(2,1)S(1)} %get-tuple-element.1241), channel_id=1, source_target_pairs={{0,8},{8,16},{16,24},{1,9},{9,17},{17,25},{2,10},{10,18},{18,26},{... | collective-permute-start | bytes 393224 | tf_op jit(solution)/shard_map/while/body/eval_jaxpr/ppermute | solution.py:15
  323.3 8.8 %collective-permute-start = (bf16[16,4096]{1,0:T(8,128)(2,1)S(1)}, bf16[16,4096]{1,0:T(8,128)(2,1)S(1)}, u32[]{:S(2)}, u32[]{:S(2)}) collective-permute-start(bf16[16,4096]{1,0:T(8,128)(2,1)S(1)} %get-tuple-element.1241), channel_id=1, source_target_pairs={{0,8},{8,16},{16,24},{1,9},{9,17},{17,25},{2,10},{10,18},{18,26},{... | collective-permute-start | bytes 393224 | tf_op jit(solution)/shard_map/while/body/eval_jaxpr/ppermute | solution.py:15
  337.8 15.7 %collective-permute-start = (bf16[16,4096]{1,0:T(8,128)(2,1)S(1)}, bf16[16,4096]{1,0:T(8,128)(2,1)S(1)}, u32[]{:S(2)}, u32[]{:S(2)}) collective-permute-start(bf16[16,4096]{1,0:T(8,128)(2,1)S(1)} %get-tuple-element.1241), channel_id=1, source_target_pairs={{0,8},{8,16},{16,24},{1,9},{9,17},{17,25},{2,10},{10,18},{18,26},{... | collective-permute-start | bytes 393224 | tf_op jit(solution)/shard_map/while/body/eval_jaxpr/ppermute | solution.py:15
  353.5 3.0 copy-start.8
  358.3 6.8 collective-permute-start.1
  367.0 11.6 %collective-permute-start.1 = (bf16[16,4096]{1,0:T(8,128)(2,1)S(1)}, bf16[16,4096]{1,0:T(8,128)(2,1)S(1)}, u32[]{:S(2)}, u32[]{:S(2)}) collective-permute-start(bf16[16,4096]{1,0:T(8,128)(2,1)S(1)} %get-tuple-element.1271), channel_id=1, source_target_pairs={{8,0},{16,8},{24,16},{9,1},{17,9},{25,17},{10,2},{18,10},{26,18},{... | collective-permute-start | bytes 393224 | tf_op jit(solution)/shard_map/while/body/eval_jaxpr/ppermute | solution.py:15
  380.4 42.8 %collective-permute-start.1 = (bf16[16,4096]{1,0:T(8,128)(2,1)S(1)}, bf16[16,4096]{1,0:T(8,128)(2,1)S(1)}, u32[]{:S(2)}, u32[]{:S(2)}) collective-permute-start(bf16[16,4096]{1,0:T(8,128)(2,1)S(1)} %get-tuple-element.1271), channel_id=1, source_target_pairs={{8,0},{16,8},{24,16},{9,1},{17,9},{25,17},{10,2},{18,10},{26,18},{... | collective-permute-start | bytes 393224 | tf_op jit(solution)/shard_map/while/body/eval_jaxpr/ppermute | solution.py:15
  426.0 8.2 %copy-start.6 = (bf16[16,4096]{1,0:T(8,128)(2,1)}, bf16[16,4096]{1,0:T(8,128)(2,1)S(1)}, u32[]{:S(2)}) copy-start(bf16[16,4096]{1,0:T(8,128)(2,1)S(1)} %fusion.11) | copy-start | bytes 393220 | tf_op jit(solution)/shard_map/while/body/eval_jaxpr/cond
  426.0 9.0 %copy-start.4 = (bf16[4096,128]{1,0:T(8,128)(2,1)S(1)}, bf16[4096,128]{1,0:T(8,128)(2,1)}, u32[]{:S(2)}) copy-start(bf16[4096,128]{1,0:T(8,128)(2,1)} %get-tuple-element.875) | copy-start | bytes 3145732 | tf_op jit(solution)/shard_map/while/body/eval_jaxpr/cond
  437.5 8.1 %collective-permute-start.1 = (bf16[16,4096]{1,0:T(8,128)(2,1)S(1)}, bf16[16,4096]{1,0:T(8,128)(2,1)S(1)}, u32[]{:S(2)}, u32[]{:S(2)}) collective-permute-start(bf16[16,4096]{1,0:T(8,128)(2,1)S(1)} %get-tuple-element.1271), channel_id=1, source_target_pairs={{8,0},{16,8},{24,16},{9,1},{17,9},{25,17},{10,2},{18,10},{26,18},{... | collective-permute-start | bytes 393224 | tf_op jit(solution)/shard_map/while/body/eval_jaxpr/ppermute | solution.py:15
  448.5 8.2 %copy-start.6 = (bf16[16,4096]{1,0:T(8,128)(2,1)}, bf16[16,4096]{1,0:T(8,128)(2,1)S(1)}, u32[]{:S(2)}) copy-start(bf16[16,4096]{1,0:T(8,128)(2,1)S(1)} %fusion.11) | copy-start | bytes 393220 | tf_op jit(solution)/shard_map/while/body/eval_jaxpr/cond
  448.5 9.0 %copy-start.4 = (bf16[4096,128]{1,0:T(8,128)(2,1)S(1)}, bf16[4096,128]{1,0:T(8,128)(2,1)}, u32[]{:S(2)}) copy-start(bf16[4096,128]{1,0:T(8,128)(2,1)} %get-tuple-element.875) | copy-start | bytes 3145732 | tf_op jit(solution)/shard_map/while/body/eval_jaxpr/cond
  460.0 8.1 %collective-permute-start.1 = (bf16[16,4096]{1,0:T(8,128)(2,1)S(1)}, bf16[16,4096]{1,0:T(8,128)(2,1)S(1)}, u32[]{:S(2)}, u32[]{:S(2)}) collective-permute-start(bf16[16,4096]{1,0:T(8,128)(2,1)S(1)} %get-tuple-element.1271), channel_id=1, source_target_pairs={{8,0},{16,8},{24,16},{9,1},{17,9},{25,17},{10,2},{18,10},{26,18},{... | collective-permute-start | bytes 393224 | tf_op jit(solution)/shard_map/while/body/eval_jaxpr/ppermute | solution.py:15
  471.0 8.2 %copy-start.6 = (bf16[16,4096]{1,0:T(8,128)(2,1)}, bf16[16,4096]{1,0:T(8,128)(2,1)S(1)}, u32[]{:S(2)}) copy-start(bf16[16,4096]{1,0:T(8,128)(2,1)S(1)} %fusion.11) | copy-start | bytes 393220 | tf_op jit(solution)/shard_map/while/body/eval_jaxpr/cond
  471.0 9.0 %copy-start.4 = (bf16[4096,128]{1,0:T(8,128)(2,1)S(1)}, bf16[4096,128]{1,0:T(8,128)(2,1)}, u32[]{:S(2)}) copy-start(bf16[4096,128]{1,0:T(8,128)(2,1)} %get-tuple-element.875) | copy-start | bytes 3145732 | tf_op jit(solution)/shard_map/while/body/eval_jaxpr/cond
  482.5 8.1 %collective-permute-start.1 = (bf16[16,4096]{1,0:T(8,128)(2,1)S(1)}, bf16[16,4096]{1,0:T(8,128)(2,1)S(1)}, u32[]{:S(2)}, u32[]{:S(2)}) collective-permute-start(bf16[16,4096]{1,0:T(8,128)(2,1)S(1)} %get-tuple-element.1271), channel_id=1, source_target_pairs={{8,0},{16,8},{24,16},{9,1},{17,9},{25,17},{10,2},{18,10},{26,18},{... | collective-permute-start | bytes 393224 | tf_op jit(solution)/shard_map/while/body/eval_jaxpr/ppermute | solution.py:15
  493.4 8.2 %copy-start.6 = (bf16[16,4096]{1,0:T(8,128)(2,1)}, bf16[16,4096]{1,0:T(8,128)(2,1)S(1)}, u32[]{:S(2)}) copy-start(bf16[16,4096]{1,0:T(8,128)(2,1)S(1)} %fusion.11) | copy-start | bytes 393220 | tf_op jit(solution)/shard_map/while/body/eval_jaxpr/cond
  493.4 9.0 %copy-start.4 = (bf16[4096,128]{1,0:T(8,128)(2,1)S(1)}, bf16[4096,128]{1,0:T(8,128)(2,1)}, u32[]{:S(2)}) copy-start(bf16[4096,128]{1,0:T(8,128)(2,1)} %get-tuple-element.875) | copy-start | bytes 3145732 | tf_op jit(solution)/shard_map/while/body/eval_jaxpr/cond
  505.0 8.1 %collective-permute-start.1 = (bf16[16,4096]{1,0:T(8,128)(2,1)S(1)}, bf16[16,4096]{1,0:T(8,128)(2,1)S(1)}, u32[]{:S(2)}, u32[]{:S(2)}) collective-permute-start(bf16[16,4096]{1,0:T(8,128)(2,1)S(1)} %get-tuple-element.1271), channel_id=1, source_target_pairs={{8,0},{16,8},{24,16},{9,1},{17,9},{25,17},{10,2},{18,10},{26,18},{... | collective-permute-start | bytes 393224 | tf_op jit(solution)/shard_map/while/body/eval_jaxpr/ppermute | solution.py:15
  515.9 8.2 %copy-start.6 = (bf16[16,4096]{1,0:T(8,128)(2,1)}, bf16[16,4096]{1,0:T(8,128)(2,1)S(1)}, u32[]{:S(2)}) copy-start(bf16[16,4096]{1,0:T(8,128)(2,1)S(1)} %fusion.11) | copy-start | bytes 393220 | tf_op jit(solution)/shard_map/while/body/eval_jaxpr/cond
  515.9 9.0 %copy-start.4 = (bf16[4096,128]{1,0:T(8,128)(2,1)S(1)}, bf16[4096,128]{1,0:T(8,128)(2,1)}, u32[]{:S(2)}) copy-start(bf16[4096,128]{1,0:T(8,128)(2,1)} %get-tuple-element.875) | copy-start | bytes 3145732 | tf_op jit(solution)/shard_map/while/body/eval_jaxpr/cond
  527.4 8.1 %collective-permute-start.1 = (bf16[16,4096]{1,0:T(8,128)(2,1)S(1)}, bf16[16,4096]{1,0:T(8,128)(2,1)S(1)}, u32[]{:S(2)}, u32[]{:S(2)}) collective-permute-start(bf16[16,4096]{1,0:T(8,128)(2,1)S(1)} %get-tuple-element.1271), channel_id=1, source_target_pairs={{8,0},{16,8},{24,16},{9,1},{17,9},{25,17},{10,2},{18,10},{26,18},{... | collective-permute-start | bytes 393224 | tf_op jit(solution)/shard_map/while/body/eval_jaxpr/ppermute | solution.py:15
  538.4 8.2 %copy-start.6 = (bf16[16,4096]{1,0:T(8,128)(2,1)}, bf16[16,4096]{1,0:T(8,128)(2,1)S(1)}, u32[]{:S(2)}) copy-start(bf16[16,4096]{1,0:T(8,128)(2,1)S(1)} %fusion.11) | copy-start | bytes 393220 | tf_op jit(solution)/shard_map/while/body/eval_jaxpr/cond
  538.4 9.0 %copy-start.4 = (bf16[4096,128]{1,0:T(8,128)(2,1)S(1)}, bf16[4096,128]{1,0:T(8,128)(2,1)}, u32[]{:S(2)}) copy-start(bf16[4096,128]{1,0:T(8,128)(2,1)} %get-tuple-element.875) | copy-start | bytes 3145732 | tf_op jit(solution)/shard_map/while/body/eval_jaxpr/cond
  549.9 8.1 %collective-permute-start.1 = (bf16[16,4096]{1,0:T(8,128)(2,1)S(1)}, bf16[16,4096]{1,0:T(8,128)(2,1)S(1)}, u32[]{:S(2)}, u32[]{:S(2)}) collective-permute-start(bf16[16,4096]{1,0:T(8,128)(2,1)S(1)} %get-tuple-element.1271), channel_id=1, source_target_pairs={{8,0},{16,8},{24,16},{9,1},{17,9},{25,17},{10,2},{18,10},{26,18},{... | collective-permute-start | bytes 393224 | tf_op jit(solution)/shard_map/while/body/eval_jaxpr/ppermute | solution.py:15
  560.9 8.2 %copy-start.6 = (bf16[16,4096]{1,0:T(8,128)(2,1)}, bf16[16,4096]{1,0:T(8,128)(2,1)S(1)}, u32[]{:S(2)}) copy-start(bf16[16,4096]{1,0:T(8,128)(2,1)S(1)} %fusion.11) | copy-start | bytes 393220 | tf_op jit(solution)/shard_map/while/body/eval_jaxpr/cond
  560.9 9.0 %copy-start.4 = (bf16[4096,128]{1,0:T(8,128)(2,1)S(1)}, bf16[4096,128]{1,0:T(8,128)(2,1)}, u32[]{:S(2)}) copy-start(bf16[4096,128]{1,0:T(8,128)(2,1)} %get-tuple-element.875) | copy-start | bytes 3145732 | tf_op jit(solution)/shard_map/while/body/eval_jaxpr/cond
  572.4 8.1 %collective-permute-start.1 = (bf16[16,4096]{1,0:T(8,128)(2,1)S(1)}, bf16[16,4096]{1,0:T(8,128)(2,1)S(1)}, u32[]{:S(2)}, u32[]{:S(2)}) collective-permute-start(bf16[16,4096]{1,0:T(8,128)(2,1)S(1)} %get-tuple-element.1271), channel_id=1, source_target_pairs={{8,0},{16,8},{24,16},{9,1},{17,9},{25,17},{10,2},{18,10},{26,18},{... | collective-permute-start | bytes 393224 | tf_op jit(solution)/shard_map/while/body/eval_jaxpr/ppermute | solution.py:15
  583.3 8.2 %copy-start.6 = (bf16[16,4096]{1,0:T(8,128)(2,1)}, bf16[16,4096]{1,0:T(8,128)(2,1)S(1)}, u32[]{:S(2)}) copy-start(bf16[16,4096]{1,0:T(8,128)(2,1)S(1)} %fusion.11) | copy-start | bytes 393220 | tf_op jit(solution)/shard_map/while/body/eval_jaxpr/cond
  583.3 9.0 %copy-start.4 = (bf16[4096,128]{1,0:T(8,128)(2,1)S(1)}, bf16[4096,128]{1,0:T(8,128)(2,1)}, u32[]{:S(2)}) copy-start(bf16[4096,128]{1,0:T(8,128)(2,1)} %get-tuple-element.875) | copy-start | bytes 3145732 | tf_op jit(solution)/shard_map/while/body/eval_jaxpr/cond
  594.9 7.5 collective-permute-start.1
  609.0 159.1 %all-gather.19.cloned.1.call-start = ((), (), s32[]{:S(2)}) async-start(), calls=%async_computation.4 | async-start | bytes 9437184 | tf_op jit(solution)/shard_map/all_gather | solution.py:201
  (12 other events, 28.7 us)
Sparse Core Ops, SparseCore 0:
  9.6 25.0 all-gather.10
  36.2 21.8 all-gather.12
  59.7 21.8 all-gather.14
  83.1 21.8 all-gather.16
  609.1 75.4 all-reduce.2
  686.0 82.0 all-gather.18
